TPU v7x, 128 devices: a whole 4x4x4 slice. The times are simulated.
128 devices in a mesh: chan: 16 (over y_lo, z, core), tile: 8 (over y_hi, x).
Axes of the slice: x: 4, y: 4 (y_hi: 2, y_lo: 2; y = y_hi * 2 + y_lo), z: 4, core: 2. Of those that a mesh axis runs over, the one named last changes fastest.
Arguments:
- voltages: bfloat16 [524288, 2048], P('chan', 'tile'), may hold values from -4 to 4
- pfb_taps: float32 [4, 2048], replicated, may hold values from -3 to 3
Outputs:
- visibility: float32 [32, 2, 2048, 2048], P('chan', None, 'tile')
All inputs are finite; a program needn't handle non-finite values.
Results may differ from a plain program's by a relative error of at most 0.0038.
Values may be sent and summed in bfloat16 or wider, within the bound.
A program may use at most 192 MiB of HBM per device.

v0:
```python
import math
import jax
import jax.numpy as jnp
from jax import lax
from jax.sharding import PartitionSpec as P

CH_DEV = 2


def from_behind(block, axis, distance):
    devices = range(lax.axis_size(axis))
    route = [(i - distance, i) for i in devices if i - distance in devices]
    return lax.ppermute(block, axis, route)


def dft_table(frame_len, channel_count):
    samples = jnp.arange(frame_len, dtype=jnp.int32)
    centers = frame_len // 8 + jnp.arange(channel_count, dtype=jnp.int32)
    phase_index = samples[:, None] * centers[None, :] % frame_len
    angle = 2.0 * jnp.pi / frame_len * phase_index.astype(jnp.float32)
    factor = 1.0 / math.sqrt(frame_len)
    return jnp.concatenate([jnp.cos(angle) * factor, -jnp.sin(angle) * factor], axis=1)


def filter_frames(pfb_taps, extended, count):
    total = pfb_taps[0][:, None] * extended[0:count]
    for tap_index in range(1, pfb_taps.shape[0]):
        total = total + pfb_taps[tap_index][:, None] * extended[tap_index : tap_index + count]
    return total


def channelize(table, pfb_taps, samples, count, block):
    tap_count = pfb_taps.shape[0]
    frame_len = pfb_taps.shape[1]
    inputs_here = samples.shape[1]

    def one_block(block_index):
        window = lax.dynamic_slice_in_dim(
            samples, block_index * block * frame_len, (block + tap_count - 1) * frame_len, 0
        )
        frames = window.astype(jnp.float32).reshape(block + tap_count - 1, frame_len, inputs_here)
        filtered = filter_frames(pfb_taps, frames, block)
        return jnp.einsum(
            "nc,sni->sci",
            table,
            filtered,
            precision=lax.Precision.HIGHEST,
            preferred_element_type=jnp.float32,
        )

    result = lax.map(one_block, jnp.arange(count // block, dtype=jnp.int32))
    return result.reshape(count, result.shape[2], inputs_here)


def shards(voltages, pfb_taps):
    chan_count = lax.axis_size("chan")
    tap_count = pfb_taps.shape[0]
    frame_len = pfb_taps.shape[1]
    inputs_here = voltages.shape[1]
    spec_here = voltages.shape[0] // frame_len
    overhang = tap_count - 1
    channels = CH_DEV * chan_count
    table = dft_table(frame_len, channels)
    leading = voltages[: overhang * frame_len]
    arrived = from_behind(leading, "chan", -1)
    extended = jnp.concatenate([voltages, arrived], axis=0)
    spectra = channelize(table, pfb_taps, extended, spec_here, 4)
    spectra = spectra.astype(jnp.bfloat16).reshape(spec_here, 2, channels, inputs_here)
    turned = lax.all_to_all(spectra, "chan", split_axis=2, concat_axis=0, tiled=True)
    total_spectra = turned.shape[0]
    products = jnp.einsum(
        "sacp,sbcq->capbq",
        turned,
        lax.all_gather(turned, "tile", axis=3, tiled=True),
        preferred_element_type=jnp.float32,
    )
    real_part = products[:, 0, :, 0, :] + products[:, 1, :, 1, :]
    imag_part = products[:, 1, :, 0, :] - products[:, 0, :, 1, :]
    return jnp.stack([real_part, imag_part], axis=1) / total_spectra


def solution(mesh):
    placed = (P("chan", "tile"), P())
    return jax.shard_map(
        shards, mesh=mesh, in_specs=placed, out_specs=P("chan", None, "tile", None), check_vma=False
    )
```

profile of v0, /device:TPU:0, one launch (start us, length us, event | category | flops | bytes accessed | tf_op | source)
XLA Modules:
  0.0 355.2 jit_solution(6156543650741576212)
XLA Ops:
  6.5 0.0 all-gather.2.cloned.1.call-start
  6.5 3.8 %slice.75 = bf16[6144,256]{1,0:T(8,128)(2,1)} slice(bf16[32768,256]{1,0:T(8,128)(2,1)} %param.4), slice={[0:6144], [0:256]} | slice | bytes 6291456 | tf_op jit(solution)/shard_map/slice | solution.py:64
  10.3 1.3 collective-permute-start
  11.6 1.1 cosine_multiply_fusion
  12.8 0.0 copy-start
  12.8 5.4 %collective-permute-done = bf16[6144,256]{1,0:T(8,128)(2,1)} collective-permute-done((bf16[6144,256]{1,0:T(8,128)(2,1)}, bf16[6144,256]{1,0:T(8,128)(2,1)}, u32[]{:S(2)}, u32[]{:S(2)}) %collective-permute-start) | collective-permute-done | bytes 3145760 | tf_op jit(solution)/shard_map/ppermute | solution.py:13
  18.2 20.0 %pad_maximum_fusion = bf16[38912,256]{1,0:T(8,128)(2,1)} fusion(bf16[6144,256]{1,0:T(8,128)(2,1)} %collective-permute-done, bf16[32768,256]{1,0:T(8,128)(2,1)} %param.4), kind=kLoop, calls=%fused_computation.16 | loop fusion | flops 39845888 | bytes 39845888 | tf_op jit(solution)/shard_map/concatenate | solution.py:66
  38.2 0.0 copy-done
  38.2 170.7 %while.12 = (s32[]{:T(128)}, bf16[4,4,64,256]{3,2,1,0:T(8,128)(2,1)S(1)}, f32[4,2048]{1,0:T(4,128)S(1)}, s32[4]{0:T(128)S(1)}, bf16[38912,256]{1,0:T(8,128)(2,1)...) while((s32[]{:T(128)}, bf16[4,4,64,256]{3,2,1,0:T(8,128)(2,1)S(1)}, ...), condition=%wide.region_1.2_spmd, body=%wide.region_0.1_spmd.sunk | while | flops 1628962816 | bytes 123568296 | solution.py:51
  38.2 0.6 dynamic_slice.17
  39.4 8.2 %dynamic-slice_convert_fusion.2 = f32[14336,256]{1,0:T(8,128)} fusion(bf16[38912,256]{1,0:T(8,128)(2,1)} %get-tuple-element.182, s32[]{:T(128)S(6)} %select_n.26), kind=kLoop, calls=%fused_computation.8.clone.1 | loop fusion | flops 3670016 | bytes 22020100 | tf_op jit(solution)/shard_map/while/body/eval_jaxpr/convert_element_type | solution.py:41
  47.7 20.9 %fusion.40 = (f32[8192,256]{1,0:T(8,128)S(1)}, f32[8192,256]{1,0:T(8,128)}, f32[8192,256]{1,0:T(8,128)}, f32[8192,256]{1,0:T(8,128)}) fusion(f32[14336,256]{1,0:T(8,128)} %dynamic-slice_convert_fusion.2), kind=kLoop, calls=%fused_computation.39.clone.1 | loop fusion | bytes 67108864 | tf_op jit(solution)/shard_map/while/body/eval_jaxpr/slice | solution.py:26
  68.7 12.2 %fusion.42 = bf16[4,4,64,256]{3,2,1,0:T(8,128)(2,1)S(1)} fusion(bf16[4,4,64,256]{3,2,1,0:T(8,128)(2,1)S(1)} %get-tuple-element.169, s32[]{:T(128)} %get-tuple-element.168, f32[4,2048,256]{2,1,0:T(8,128)} %bitcast.70, f32[4,2048,256]{2,1,0:T(8,128)} %bitcast.71, f32[4,2048,256]{2,1,0:T(8,128)} %bitcast.72, f32[4,2048,256]{2,1,0:T(8,128)S(1)} %bitcast.69, ...), kind=kOutput, calls=%fused_computation.14.clone.1 | convolution fusion | flops 1625292800 | bytes 34373636 | tf_op jit(solution)/shard_map/while/body/eval_jaxpr/nc,sni->sci/dot_general | solution.py:43
  80.9 0.6 dynamic_slice.17
  82.1 8.2 %dynamic-slice_convert_fusion.2 = f32[14336,256]{1,0:T(8,128)} fusion(bf16[38912,256]{1,0:T(8,128)(2,1)} %get-tuple-element.182, s32[]{:T(128)S(6)} %select_n.26), kind=kLoop, calls=%fused_computation.8.clone.1 | loop fusion | flops 3670016 | bytes 22020100 | tf_op jit(solution)/shard_map/while/body/eval_jaxpr/convert_element_type | solution.py:41
  90.4 20.9 %fusion.40 = (f32[8192,256]{1,0:T(8,128)S(1)}, f32[8192,256]{1,0:T(8,128)}, f32[8192,256]{1,0:T(8,128)}, f32[8192,256]{1,0:T(8,128)}) fusion(f32[14336,256]{1,0:T(8,128)} %dynamic-slice_convert_fusion.2), kind=kLoop, calls=%fused_computation.39.clone.1 | loop fusion | bytes 67108864 | tf_op jit(solution)/shard_map/while/body/eval_jaxpr/slice | solution.py:26
  111.3 12.2 %fusion.42 = bf16[4,4,64,256]{3,2,1,0:T(8,128)(2,1)S(1)} fusion(bf16[4,4,64,256]{3,2,1,0:T(8,128)(2,1)S(1)} %get-tuple-element.169, s32[]{:T(128)} %get-tuple-element.168, f32[4,2048,256]{2,1,0:T(8,128)} %bitcast.70, f32[4,2048,256]{2,1,0:T(8,128)} %bitcast.71, f32[4,2048,256]{2,1,0:T(8,128)} %bitcast.72, f32[4,2048,256]{2,1,0:T(8,128)S(1)} %bitcast.69, ...), kind=kOutput, calls=%fused_computation.14.clone.1 | convolution fusion | flops 1625292800 | bytes 34373636 | tf_op jit(solution)/shard_map/while/body/eval_jaxpr/nc,sni->sci/dot_general | solution.py:43
  123.6 0.6 dynamic_slice.17
  124.8 8.2 %dynamic-slice_convert_fusion.2 = f32[14336,256]{1,0:T(8,128)} fusion(bf16[38912,256]{1,0:T(8,128)(2,1)} %get-tuple-element.182, s32[]{:T(128)S(6)} %select_n.26), kind=kLoop, calls=%fused_computation.8.clone.1 | loop fusion | flops 3670016 | bytes 22020100 | tf_op jit(solution)/shard_map/while/body/eval_jaxpr/convert_element_type | solution.py:41
  133.1 20.9 %fusion.40 = (f32[8192,256]{1,0:T(8,128)S(1)}, f32[8192,256]{1,0:T(8,128)}, f32[8192,256]{1,0:T(8,128)}, f32[8192,256]{1,0:T(8,128)}) fusion(f32[14336,256]{1,0:T(8,128)} %dynamic-slice_convert_fusion.2), kind=kLoop, calls=%fused_computation.39.clone.1 | loop fusion | bytes 67108864 | tf_op jit(solution)/shard_map/while/body/eval_jaxpr/slice | solution.py:26
  154.0 12.2 %fusion.42 = bf16[4,4,64,256]{3,2,1,0:T(8,128)(2,1)S(1)} fusion(bf16[4,4,64,256]{3,2,1,0:T(8,128)(2,1)S(1)} %get-tuple-element.169, s32[]{:T(128)} %get-tuple-element.168, f32[4,2048,256]{2,1,0:T(8,128)} %bitcast.70, f32[4,2048,256]{2,1,0:T(8,128)} %bitcast.71, f32[4,2048,256]{2,1,0:T(8,128)} %bitcast.72, f32[4,2048,256]{2,1,0:T(8,128)S(1)} %bitcast.69, ...), kind=kOutput, calls=%fused_computation.14.clone.1 | convolution fusion | flops 1625292800 | bytes 34373636 | tf_op jit(solution)/shard_map/while/body/eval_jaxpr/nc,sni->sci/dot_general | solution.py:43
  166.2 0.6 dynamic_slice.17
  167.5 8.2 %dynamic-slice_convert_fusion.2 = f32[14336,256]{1,0:T(8,128)} fusion(bf16[38912,256]{1,0:T(8,128)(2,1)} %get-tuple-element.182, s32[]{:T(128)S(6)} %select_n.26), kind=kLoop, calls=%fused_computation.8.clone.1 | loop fusion | flops 3670016 | bytes 22020100 | tf_op jit(solution)/shard_map/while/body/eval_jaxpr/convert_element_type | solution.py:41
  175.7 20.9 %fusion.40 = (f32[8192,256]{1,0:T(8,128)S(1)}, f32[8192,256]{1,0:T(8,128)}, f32[8192,256]{1,0:T(8,128)}, f32[8192,256]{1,0:T(8,128)}) fusion(f32[14336,256]{1,0:T(8,128)} %dynamic-slice_convert_fusion.2), kind=kLoop, calls=%fused_computation.39.clone.1 | loop fusion | bytes 67108864 | tf_op jit(solution)/shard_map/while/body/eval_jaxpr/slice | solution.py:26
  196.7 12.2 %fusion.42 = bf16[4,4,64,256]{3,2,1,0:T(8,128)(2,1)S(1)} fusion(bf16[4,4,64,256]{3,2,1,0:T(8,128)(2,1)S(1)} %get-tuple-element.169, s32[]{:T(128)} %get-tuple-element.168, f32[4,2048,256]{2,1,0:T(8,128)} %bitcast.70, f32[4,2048,256]{2,1,0:T(8,128)} %bitcast.71, f32[4,2048,256]{2,1,0:T(8,128)} %bitcast.72, f32[4,2048,256]{2,1,0:T(8,128)S(1)} %bitcast.69, ...), kind=kOutput, calls=%fused_computation.14.clone.1 | convolution fusion | flops 1625292800 | bytes 34373636 | tf_op jit(solution)/shard_map/while/body/eval_jaxpr/nc,sni->sci/dot_general | solution.py:43
  208.9 0.3 copy.19
  209.2 48.7 %all_to_all.18 = bf16[16,2,32,256]{3,0,1,2:T(8,128)(2,1)S(1)} all-to-all(bf16[16,2,32,256]{3,0,1,2:T(8,128)(2,1)S(1)} %copy.19), channel_id=1, replica_groups=mesh['chan'=16,'tile'=8] {'chan'}, dimensions={2} | all-to-all | bytes 1048576 | tf_op jit(solution)/shard_map/all_to_all | solution.py:69
  258.0 0.8 copy.21
  258.8 0.0 all-gather.2.cloned.1.call-update
  258.8 77.6 %all-gather.2.cloned.1.call-done = bf16[256,2,2,2048]{3,0,1,2:T(8,128)(2,1)} async-done(((bf16[256,2,2,256]{3,0,1,2:T(8,128)(2,1)}), bf16[256,2,2,2048]{3,0,1,2:T(8,128)(2,1)}) %all-gather.2.cloned.1.call-update) | async-done | bytes 4194320 | tf_op jit(solution)/shard_map/all_gather | solution.py:74
  336.4 4.7 %fusion.22 = f32[2,2,256,2,2048]{4,2,3,1,0:T(8,128)S(1)} fusion(bf16[256,2,2,256,1]{3,0,4,1,2:T(8,128)(2,1)} %bitcast.74, bf16[256,2,2,2048]{3,0,1,2:T(8,128)(2,1)} %all-gather.2.cloned.1.call-done), kind=kOutput, calls=%fused_computation.24 | convolution fusion | flops 2147483648 | bytes 21495808 | tf_op jit(solution)/shard_map/sacp,sbcq->capbq/dot_general | solution.py:71
  341.1 0.8 fusion.19
  341.9 0.8 fusion.21
  342.7 1.6 maximum_multiply_fusion
  344.3 4.0 %copy.25 = f32[2,2,256,2048]{3,2,1,0:T(8,128)} copy(f32[2,2,256,2048]{3,2,0,1:T(8,128)S(1)} %maximum_multiply_fusion) | data formatting | bytes 16777216 | tf_op jit(solution)/shard_map/div | solution.py:79
  (8 shorter events, 0.1 us)
Async XLA Ops:
  6.5 329.9 %all-gather.2.cloned.1.call-start = ((), (), s32[]{:S(2)}) async-start(), calls=%async_computation.1 | async-start | bytes 4718592 | tf_op jit(solution)/shard_map/all_gather | solution.py:74
  10.3 7.9 %collective-permute-start = (bf16[6144,256]{1,0:T(8,128)(2,1)}, bf16[6144,256]{1,0:T(8,128)(2,1)}, u32[]{:S(2)}, u32[]{:S(2)}) collective-permute-start(bf16[6144,256]{1,0:T(8,128)(2,1)} %slice.75), channel_id=1, source_target_pairs={{8,0},{16,8},{24,16},{32,24},{40,32},{48,40},{56,48},{64,56},{72,6... | collective-permute-start | bytes 9437192 | tf_op jit(solution)/shard_map/ppermute | solution.py:13
  12.8 25.4 %copy-start = (f32[4,2048]{1,0:T(4,128)S(1)}, f32[4,2048]{1,0:T(4,128)}, u32[]{:S(2)}) copy-start(f32[4,2048]{1,0:T(4,128)} %param.5) | copy-start | bytes 98308
Sparse Core Ops, SparseCore 0:
  258.9 77.4 all-gather.1
where the time goes:
time: 356 us; the launch traced here: 355 us
  local copies, waits for them, and re-layouts  95.1 us (27%)
  waiting for transfers between devices  83 us (23%)
  other arithmetic  57.3 us (16%)
  matrix products  53.5 us (15%)
  blocking collectives  48.7 us (14%)
  between operations  13.5 us (4%)
    slice x8, local copies, waits for them, and re-layouts, filter_frames(): total = pfb_taps[0][:, None] * extended[0:count]  83.9 us
    all_gather x1, waiting for transfers between devices, shards(): lax.all_gather(turned, 'tile', axis=3, tiled=True)  77.6 us
    dot_general x4, matrix products, one_block(): jnp.einsum('nc,sni->sci', table, filtered, precision=lax.Precision.HIGHES...  48.8 us
    all_to_all x1, blocking collectives, shards(): lax.all_to_all(spectra, 'chan', split_axis=2, concat_axis=0, tiled=True)  48.7 us
    convert_element_type x4, other arithmetic, one_block(): window.astype(jnp.float32)  33 us
    concatenate x1, other arithmetic, shards(): extended = jnp.concatenate([voltages, arrived], axis=0)  20 us
  transfers between devices with their start and end apart: 2, of which 2 were waited for; matrix products, arithmetic and copies ran while one was open for 0% of the time, Pallas kernels for 0%

commit v1 on v0

--- a/solution.py
+++ b/solution.py
@@ -66,7 +66,10 @@
     extended = jnp.concatenate([voltages, arrived], axis=0)
     spectra = channelize(table, pfb_taps, extended, spec_here, 4)
     spectra = spectra.astype(jnp.bfloat16).reshape(spec_here, 2, channels, inputs_here)
-    turned = lax.all_to_all(spectra, "chan", split_axis=2, concat_axis=0, tiled=True)
+    turned = jnp.concatenate(
+        lax.all_to_all(jnp.stack(jnp.split(spectra, lax.axis_size("chan"), axis=2)), "chan", 0, 0),
+        axis=0,
+    )
     total_spectra = turned.shape[0]
     products = jnp.einsum(
         "sacp,sbcq->capbq",

time: 356 us -> 356 us (level)
  no operation moved by 1% of the time
where the time goes in v1:
time: 356 us
  local copies, waits for them, and re-layouts  95.6 us (27%)
  waiting for transfers between devices  83 us (23%)
  other arithmetic  57.3 us (16%)
  matrix products  53.5 us (15%)
  blocking collectives  48.7 us (14%)
  between operations  13.5 us (4%)
    slice x8, local copies, waits for them, and re-layouts, filter_frames(): total = pfb_taps[0][:, None] * extended[0:count]  83.9 us
    all_gather x1, waiting for transfers between devices, shards(): lax.all_gather(turned, 'tile', axis=3, tiled=True)  77.6 us
    dot_general x4, matrix products, one_block(): jnp.einsum('nc,sni->sci', table, filtered, precision=lax.Precision.HIGHES...  48.8 us
    all_to_all x1, blocking collectives, shards(): lax.all_to_all(jnp.stack(jnp.split(spectra, lax.axis_size('chan'), axis=2...  48.7 us
    convert_element_type x4, other arithmetic, one_block(): window.astype(jnp.float32)  33 us
    concatenate x1, other arithmetic, shards(): extended = jnp.concatenate([voltages, arrived], axis=0)  20 us
  transfers between devices with their start and end apart: 2, of which 2 were waited for; matrix products, arithmetic and copies ran while one was open for 0% of the time, Pallas kernels for 0%

profile of v1, /device:TPU:0, one launch (start us, length us, event | category | flops | bytes accessed | tf_op | source)
XLA Modules:
  0.0 355.7 jit_solution(12858709111550241225)
XLA Ops:
  6.5 0.0 all-gather.2.cloned.1.call-start
  6.5 3.8 %slice.75 = bf16[6144,256]{1,0:T(8,128)(2,1)} slice(bf16[32768,256]{1,0:T(8,128)(2,1)} %param.4), slice={[0:6144], [0:256]} | slice | bytes 6291456 | tf_op jit(solution)/shard_map/slice | solution.py:64
  10.3 1.3 collective-permute-start
  11.6 1.1 cosine_multiply_fusion
  12.8 0.0 copy-start
  12.8 5.4 %collective-permute-done = bf16[6144,256]{1,0:T(8,128)(2,1)} collective-permute-done((bf16[6144,256]{1,0:T(8,128)(2,1)}, bf16[6144,256]{1,0:T(8,128)(2,1)}, u32[]{:S(2)}, u32[]{:S(2)}) %collective-permute-start) | collective-permute-done | bytes 3145760 | tf_op jit(solution)/shard_map/ppermute | solution.py:13
  18.2 20.0 %pad_maximum_fusion = bf16[38912,256]{1,0:T(8,128)(2,1)} fusion(bf16[6144,256]{1,0:T(8,128)(2,1)} %collective-permute-done, bf16[32768,256]{1,0:T(8,128)(2,1)} %param.4), kind=kLoop, calls=%fused_computation.16 | loop fusion | flops 39845888 | bytes 39845888 | tf_op jit(solution)/shard_map/concatenate | solution.py:66
  38.2 0.0 copy-done
  38.2 170.7 %while.12 = (s32[]{:T(128)}, bf16[4,4,64,256]{3,2,1,0:T(8,128)(2,1)S(1)}, f32[4,2048]{1,0:T(4,128)S(1)}, s32[4]{0:T(128)S(1)}, bf16[38912,256]{1,0:T(8,128)(2,1)...) while((s32[]{:T(128)}, bf16[4,4,64,256]{3,2,1,0:T(8,128)(2,1)S(1)}, ...), condition=%wide.region_1.2_spmd, body=%wide.region_0.1_spmd.sunk | while | flops 1628962816 | bytes 123568296 | solution.py:51
  38.2 0.6 dynamic_slice.17
  39.4 8.2 %dynamic-slice_convert_fusion.2 = f32[14336,256]{1,0:T(8,128)} fusion(bf16[38912,256]{1,0:T(8,128)(2,1)} %get-tuple-element.182, s32[]{:T(128)S(6)} %select_n.26), kind=kLoop, calls=%fused_computation.8.clone.1 | loop fusion | flops 3670016 | bytes 22020100 | tf_op jit(solution)/shard_map/while/body/eval_jaxpr/convert_element_type | solution.py:41
  47.7 20.9 %fusion.40 = (f32[8192,256]{1,0:T(8,128)S(1)}, f32[8192,256]{1,0:T(8,128)}, f32[8192,256]{1,0:T(8,128)}, f32[8192,256]{1,0:T(8,128)}) fusion(f32[14336,256]{1,0:T(8,128)} %dynamic-slice_convert_fusion.2), kind=kLoop, calls=%fused_computation.71.clone.1 | loop fusion | bytes 67108864 | tf_op jit(solution)/shard_map/while/body/eval_jaxpr/slice | solution.py:26
  68.7 12.2 %fusion.42 = bf16[4,4,64,256]{3,2,1,0:T(8,128)(2,1)S(1)} fusion(bf16[4,4,64,256]{3,2,1,0:T(8,128)(2,1)S(1)} %get-tuple-element.169, s32[]{:T(128)} %get-tuple-element.168, f32[4,2048,256]{2,1,0:T(8,128)} %bitcast.131, f32[4,2048,256]{2,1,0:T(8,128)} %bitcast.132, f32[4,2048,256]{2,1,0:T(8,128)} %bitcast.133, f32[4,2048,256]{2,1,0:T(8,128)S(1)} %bitcast.130, ...), kind=kOutput, calls=%fused_computation.14.clone.1 | convolution fusion | flops 1625292800 | bytes 34373636 | tf_op jit(solution)/shard_map/while/body/eval_jaxpr/nc,sni->sci/dot_general | solution.py:43
  80.9 0.6 dynamic_slice.17
  82.1 8.2 %dynamic-slice_convert_fusion.2 = f32[14336,256]{1,0:T(8,128)} fusion(bf16[38912,256]{1,0:T(8,128)(2,1)} %get-tuple-element.182, s32[]{:T(128)S(6)} %select_n.26), kind=kLoop, calls=%fused_computation.8.clone.1 | loop fusion | flops 3670016 | bytes 22020100 | tf_op jit(solution)/shard_map/while/body/eval_jaxpr/convert_element_type | solution.py:41
  90.4 20.9 %fusion.40 = (f32[8192,256]{1,0:T(8,128)S(1)}, f32[8192,256]{1,0:T(8,128)}, f32[8192,256]{1,0:T(8,128)}, f32[8192,256]{1,0:T(8,128)}) fusion(f32[14336,256]{1,0:T(8,128)} %dynamic-slice_convert_fusion.2), kind=kLoop, calls=%fused_computation.71.clone.1 | loop fusion | bytes 67108864 | tf_op jit(solution)/shard_map/while/body/eval_jaxpr/slice | solution.py:26
  111.3 12.2 %fusion.42 = bf16[4,4,64,256]{3,2,1,0:T(8,128)(2,1)S(1)} fusion(bf16[4,4,64,256]{3,2,1,0:T(8,128)(2,1)S(1)} %get-tuple-element.169, s32[]{:T(128)} %get-tuple-element.168, f32[4,2048,256]{2,1,0:T(8,128)} %bitcast.131, f32[4,2048,256]{2,1,0:T(8,128)} %bitcast.132, f32[4,2048,256]{2,1,0:T(8,128)} %bitcast.133, f32[4,2048,256]{2,1,0:T(8,128)S(1)} %bitcast.130, ...), kind=kOutput, calls=%fused_computation.14.clone.1 | convolution fusion | flops 1625292800 | bytes 34373636 | tf_op jit(solution)/shard_map/while/body/eval_jaxpr/nc,sni->sci/dot_general | solution.py:43
  123.6 0.6 dynamic_slice.17
  124.8 8.2 %dynamic-slice_convert_fusion.2 = f32[14336,256]{1,0:T(8,128)} fusion(bf16[38912,256]{1,0:T(8,128)(2,1)} %get-tuple-element.182, s32[]{:T(128)S(6)} %select_n.26), kind=kLoop, calls=%fused_computation.8.clone.1 | loop fusion | flops 3670016 | bytes 22020100 | tf_op jit(solution)/shard_map/while/body/eval_jaxpr/convert_element_type | solution.py:41
  133.1 20.9 %fusion.40 = (f32[8192,256]{1,0:T(8,128)S(1)}, f32[8192,256]{1,0:T(8,128)}, f32[8192,256]{1,0:T(8,128)}, f32[8192,256]{1,0:T(8,128)}) fusion(f32[14336,256]{1,0:T(8,128)} %dynamic-slice_convert_fusion.2), kind=kLoop, calls=%fused_computation.71.clone.1 | loop fusion | bytes 67108864 | tf_op jit(solution)/shard_map/while/body/eval_jaxpr/slice | solution.py:26
  154.0 12.2 %fusion.42 = bf16[4,4,64,256]{3,2,1,0:T(8,128)(2,1)S(1)} fusion(bf16[4,4,64,256]{3,2,1,0:T(8,128)(2,1)S(1)} %get-tuple-element.169, s32[]{:T(128)} %get-tuple-element.168, f32[4,2048,256]{2,1,0:T(8,128)} %bitcast.131, f32[4,2048,256]{2,1,0:T(8,128)} %bitcast.132, f32[4,2048,256]{2,1,0:T(8,128)} %bitcast.133, f32[4,2048,256]{2,1,0:T(8,128)S(1)} %bitcast.130, ...), kind=kOutput, calls=%fused_computation.14.clone.1 | convolution fusion | flops 1625292800 | bytes 34373636 | tf_op jit(solution)/shard_map/while/body/eval_jaxpr/nc,sni->sci/dot_general | solution.py:43
  166.2 0.6 dynamic_slice.17
  167.5 8.2 %dynamic-slice_convert_fusion.2 = f32[14336,256]{1,0:T(8,128)} fusion(bf16[38912,256]{1,0:T(8,128)(2,1)} %get-tuple-element.182, s32[]{:T(128)S(6)} %select_n.26), kind=kLoop, calls=%fused_computation.8.clone.1 | loop fusion | flops 3670016 | bytes 22020100 | tf_op jit(solution)/shard_map/while/body/eval_jaxpr/convert_element_type | solution.py:41
  175.7 20.9 %fusion.40 = (f32[8192,256]{1,0:T(8,128)S(1)}, f32[8192,256]{1,0:T(8,128)}, f32[8192,256]{1,0:T(8,128)}, f32[8192,256]{1,0:T(8,128)}) fusion(f32[14336,256]{1,0:T(8,128)} %dynamic-slice_convert_fusion.2), kind=kLoop, calls=%fused_computation.71.clone.1 | loop fusion | bytes 67108864 | tf_op jit(solution)/shard_map/while/body/eval_jaxpr/slice | solution.py:26
  196.7 12.2 %fusion.42 = bf16[4,4,64,256]{3,2,1,0:T(8,128)(2,1)S(1)} fusion(bf16[4,4,64,256]{3,2,1,0:T(8,128)(2,1)S(1)} %get-tuple-element.169, s32[]{:T(128)} %get-tuple-element.168, f32[4,2048,256]{2,1,0:T(8,128)} %bitcast.131, f32[4,2048,256]{2,1,0:T(8,128)} %bitcast.132, f32[4,2048,256]{2,1,0:T(8,128)} %bitcast.133, f32[4,2048,256]{2,1,0:T(8,128)S(1)} %bitcast.130, ...), kind=kOutput, calls=%fused_computation.14.clone.1 | convolution fusion | flops 1625292800 | bytes 34373636 | tf_op jit(solution)/shard_map/while/body/eval_jaxpr/nc,sni->sci/dot_general | solution.py:43
  209.7 0.1 copy.28
  209.8 48.7 %all_to_all.5 = bf16[16,16,2,2,256]{4,1,2,3,0:T(8,128)(2,1)S(1)} all-to-all(bf16[16,16,2,2,256]{4,1,2,3,0:T(8,128)(2,1)S(1)} %copy.28), channel_id=1, replica_groups=mesh['chan'=16,'tile'=8] {'chan'}, dimensions={0} | all-to-all | bytes 1048576 | tf_op jit(solution)/shard_map/all_to_all | solution.py:70
  258.5 0.8 copy.29
  259.3 0.0 all-gather.2.cloned.1.call-update
  259.4 77.6 %all-gather.2.cloned.1.call-done = bf16[256,2,2,2048]{3,0,1,2:T(8,128)(2,1)} async-done(((bf16[256,2,2,256]{3,0,1,2:T(8,128)(2,1)}), bf16[256,2,2,2048]{3,0,1,2:T(8,128)(2,1)}) %all-gather.2.cloned.1.call-update) | async-done | bytes 4194320 | tf_op jit(solution)/shard_map/all_gather | solution.py:77
  336.9 4.7 %fusion.22 = f32[2,2,256,2,2048]{4,2,3,1,0:T(8,128)S(1)} fusion(bf16[256,2,2,256,1]{3,0,4,1,2:T(8,128)(2,1)} %bitcast.135, bf16[256,2,2,2048]{3,0,1,2:T(8,128)(2,1)} %all-gather.2.cloned.1.call-done), kind=kOutput, calls=%fused_computation.24 | convolution fusion | flops 2147483648 | bytes 21495808 | tf_op jit(solution)/shard_map/sacp,sbcq->capbq/dot_general | solution.py:74
  341.7 0.8 fusion.19
  342.4 0.8 fusion.21
  343.2 1.6 maximum_multiply_fusion
  344.9 4.0 %copy.33 = f32[2,2,256,2048]{3,2,1,0:T(8,128)} copy(f32[2,2,256,2048]{3,2,0,1:T(8,128)S(1)} %maximum_multiply_fusion) | data formatting | bytes 16777216 | tf_op jit(solution)/shard_map/div | solution.py:82
  (24 shorter events, 0.8 us)
Async XLA Ops:
  6.5 330.4 %all-gather.2.cloned.1.call-start = ((), (), s32[]{:S(2)}) async-start(), calls=%async_computation.1 | async-start | bytes 4718592 | tf_op jit(solution)/shard_map/all_gather | solution.py:77
  10.3 7.9 %collective-permute-start = (bf16[6144,256]{1,0:T(8,128)(2,1)}, bf16[6144,256]{1,0:T(8,128)(2,1)}, u32[]{:S(2)}, u32[]{:S(2)}) collective-permute-start(bf16[6144,256]{1,0:T(8,128)(2,1)} %slice.75), channel_id=1, source_target_pairs={{8,0},{16,8},{24,16},{32,24},{40,32},{48,40},{56,48},{64,56},{72,6... | collective-permute-start | bytes 9437192 | tf_op jit(solution)/shard_map/ppermute | solution.py:13
  12.8 25.4 %copy-start = (f32[4,2048]{1,0:T(4,128)S(1)}, f32[4,2048]{1,0:T(4,128)}, u32[]{:S(2)}) copy-start(f32[4,2048]{1,0:T(4,128)} %param.5) | copy-start | bytes 98308
Sparse Core Ops, SparseCore 0:
  259.5 77.4 all-gather.1
